TPU v7x, 256 devices: a whole 4x4x8 slice. The times are simulated.
256 devices in a mesh: seq: 64 (over x, z, core), head: 4 (over y).
Axes of the slice: x: 4, y: 4, z: 8, core: 2. Of those that a mesh axis runs over, the one named last changes fastest.
Arguments:
- tokens: bfloat16 [21504, 4096], P('seq', 'head')
- w_short: float32 [3, 4096], P(None, 'head'), may hold values from 0.25 to 1.5
- w_query: bfloat16 [4096, 2048], P(None, 'head')
- w_key: bfloat16 [4096, 2048], P(None, 'head')
- w_value: bfloat16 [4096, 2048], P(None, 'head'), may hold values from -0.09375 to 0.09375
- owner_lengths: int32 [64], replicated, may hold values from 1 to 224, as said below
Outputs:
- attended: bfloat16 [14336, 2048], P('seq', 'head')
Inputs may be any that keep to these rules, and one draw needn't show every extreme that they name: The counts sum to 7168; owner o holds the coarse rows from starts[o] on, with o * 112 <= starts[o] and starts[o] + owner_lengths[o] <= (o + 2) * 112; the largest count is exactly 224.
All inputs are finite; a program needn't handle non-finite values.
Results may differ from a plain program's by a relative error of at most 0.012.
The roundings to bfloat16 on the way count: a program that leaves them out, or rounds other values in their place, can miss the bound.
Values may be sent and summed in bfloat16 or wider, within the bound.
A program may use at most 128 MiB of HBM per device.

v0:
```python
import math
import jax
import jax.numpy as jnp
from jax import lax
from jax.sharding import PartitionSpec as P

HD = 128
masked_score = -1e30


def from_behind(x, axis, by):
    devices = lax.axis_size(axis)
    pairs = [(i, i + by) for i in range(devices) if 0 <= i + by < devices]
    return lax.ppermute(x, axis, pairs)


def block_scores(owned, key_block, offset, query_pos):
    length = key_block.shape[0]
    keyed = key_block.reshape(length, owned.shape[1], HD)
    scores = jnp.einsum("qhd,khd->hqk", owned, keyed, preferred_element_type=jnp.float32) * (
        1.0 / math.sqrt(HD)
    )
    key_pos = offset + jnp.arange(length, dtype=jnp.int32)
    allowed = key_pos[None, :] <= query_pos[:, None]
    return jnp.where(allowed[None], scores, masked_score)


def block_context(owned, key_block, value_block, offset, query_pos, maxima):
    scores = block_scores(owned, key_block, offset, query_pos)
    weights = jnp.exp(scores - maxima[:, :, None])
    length = value_block.shape[0]
    valued = value_block.reshape(length, owned.shape[1], HD)
    added = jnp.einsum(
        "hqk,khd->hqd", weights.astype(jnp.bfloat16), valued, preferred_element_type=jnp.float32
    )
    return (jnp.sum(weights, axis=2), added)


def shards(tokens, w_short, w_query, w_key, w_value, owner_lengths):
    rows_local = tokens.shape[0]
    coarse_local = rows_local // 3
    width_part = tokens.shape[1]
    seq_count = lax.axis_size("seq")
    position = lax.axis_index("seq")
    boundary = from_behind(tokens[rows_local - 2 :], "seq", 1)
    shifted = jnp.concatenate([boundary, tokens[: rows_local - 2]], axis=0)
    grouped = shifted.reshape(coarse_local, 3, width_part)
    pooled = (
        grouped[:, 0].astype(jnp.float32) * w_short[0]
        + grouped[:, 1].astype(jnp.float32) * w_short[1]
        + grouped[:, 2].astype(jnp.float32) * w_short[2]
    )
    squares = lax.psum(jnp.sum(pooled * pooled, axis=1), "head")
    full_width = width_part * lax.axis_size("head")
    norm_scale = lax.rsqrt(squares / full_width + 1e-05)
    coarse_part = (pooled * norm_scale[:, None]).astype(jnp.bfloat16)
    features = w_query.shape[1]
    zero_sums = jnp.zeros((coarse_local, features), jnp.float32)
    carried = (zero_sums, zero_sums, zero_sums)
    shard_rows = lax.all_gather(coarse_part, "head", axis=1, tiled=True)
    outputs = []
    for running, weight in zip(carried, (w_query, w_key, w_value)):
        outputs.append(jnp.dot(shard_rows, weight, preferred_element_type=jnp.float32))
    query_sum, key_sum, value_sum = tuple(outputs)
    queries = query_sum.astype(jnp.bfloat16)
    key_rows = key_sum.astype(jnp.bfloat16)
    value_rows = value_sum.astype(jnp.bfloat16)
    starts = jnp.cumsum(owner_lengths) - owner_lengths
    owners = jnp.arange(seq_count, dtype=jnp.int32)
    chosen = owners == position
    first_row = jnp.sum(jnp.where(chosen, starts, 0))
    row_count = jnp.sum(jnp.where(chosen, owner_lengths, 0))
    capacity = 2 * coarse_local
    following = from_behind(queries, "seq", -1)
    window = jnp.concatenate(
        [queries, following, jnp.zeros((coarse_local, features), jnp.bfloat16)], axis=0
    )
    local_start = first_row - position * coarse_local
    owned_rows = lax.dynamic_slice_in_dim(window, local_start, capacity, 0)
    head_count = features // HD
    owned = owned_rows.reshape(capacity, head_count, HD)
    query_pos = first_row + jnp.arange(capacity, dtype=jnp.int32)
    last_row = first_row + row_count
    coarse_total = seq_count * coarse_local
    start_max = jnp.full((head_count, capacity), masked_score, jnp.float32)
    start_sums = (
        jnp.zeros((head_count, capacity), jnp.float32),
        jnp.zeros((head_count, capacity, HD), jnp.float32),
    )
    key_all, value_all = (
        lax.all_gather(key_rows, "seq", axis=0, tiled=True),
        lax.all_gather(value_rows, "seq", axis=0, tiled=True),
    )
    block_size = math.gcd(coarse_total, 512)
    blocks = (last_row + block_size - 1) // block_size

    def find_max(index, maxima):
        key_block = lax.dynamic_slice_in_dim(key_all, index * block_size, block_size, 0)
        return jnp.maximum(
            maxima, jnp.max(block_scores(owned, key_block, index * block_size, query_pos), axis=2)
        )

    maxima = lax.fori_loop(0, blocks, find_max, start_max)

    def add_block(index, carried):
        offset = index * block_size
        key_block = lax.dynamic_slice_in_dim(key_all, offset, block_size, 0)
        value_block = lax.dynamic_slice_in_dim(value_all, offset, block_size, 0)
        sums, added = block_context(owned, key_block, value_block, offset, query_pos, maxima)
        return (carried[0] + sums, carried[1] + added)

    totals, context = lax.fori_loop(0, blocks, add_block, start_sums)
    result = (context / totals[:, :, None]).transpose(1, 0, 2).reshape(capacity, features)
    live = jnp.arange(capacity, dtype=jnp.int32) < row_count
    return jnp.where(live[:, None], result, 0.0).astype(jnp.bfloat16)


def solution(mesh):
    return jax.shard_map(
        shards,
        mesh=mesh,
        in_specs=(
            P("seq", "head"),
            P(None, "head"),
            P(None, "head"),
            P(None, "head"),
            P(None, "head"),
            P(),
        ),
        out_specs=P("seq", "head"),
        check_vma=False,
    )
```

profile of v0, /device:TPU:199, one launch (start us, length us, event | category | flops | bytes accessed | tf_op | source)
XLA Modules:
  0.0 273.7 jit_solution(7263793353940745998)
XLA Ops:
  7.3 3.2 %collective-permute-start = (bf16[2,1024]{1,0:T(2,128)(2,1)S(1)}, bf16[2,1024]{1,0:T(2,128)(2,1)S(1)}, u32[]{:S(2)}, u32[]{:S(2)}) collective-permute-start(bf16[2,1024]{1,0:T(2,128)(2,1)S(1)} %slice.24), channel_id=1, source_target_pairs={{0,4},{4,8},{8,12},{12,16},{16,20},{20,24},{24,28},{28,32},{32,36}... | collective-permute-start | bytes 12296 | tf_op jit(solution)/shard_map/ppermute | solution.py:14
  11.3 1.3 pad_maximum_fusion
  14.4 8.7 %psum.7 = f32[112]{0:T(128)S(1)} all-reduce(f32[112]{0:T(128)S(1)} %get-tuple-element.175), channel_id=1, replica_groups=mesh['seq'=64,'head'=4] {'head'}, use_global_device_ids=true, to_apply=%region_4.5 | all-reduce | flops 112 | bytes 896 | tf_op jit(solution)/shard_map/psum | solution.py:53
  23.3 12.6 %all_gather.9 = bf16[112,4096]{1,0:T(8,128)(2,1)S(1)} all-gather(bf16[112,1024]{1,0:T(8,128)(2,1)S(1)} %multiply_convert_fusion), channel_id=1, replica_groups=mesh['seq'=64,'head'=4] {'head'}, dimensions={1}, use_global_device_ids=true | all-gather | bytes 1146880 | tf_op jit(solution)/shard_map/all_gather | solution.py:60
  35.9 3.6 %convolution_convert_fusion.2 = bf16[112,512]{1,0:T(8,128)(2,1)} fusion(bf16[112,4096]{1,0:T(8,128)(2,1)S(1)} %all_gather.9, bf16[4096,512]{1,0:T(8,128)(2,1)} %param.13), kind=kOutput, calls=%fused_computation.20 | convolution fusion | flops 469819392 | bytes 5226496 | tf_op jit(solution)/shard_map/dot_general | solution.py:63
  39.6 3.6 %convolution_convert_fusion = bf16[112,512]{1,0:T(8,128)(2,1)} fusion(bf16[112,4096]{1,0:T(8,128)(2,1)S(1)} %all_gather.9, bf16[4096,512]{1,0:T(8,128)(2,1)} %param.14), kind=kOutput, calls=%fused_computation.18 | convolution fusion | flops 469819392 | bytes 5226496 | tf_op jit(solution)/shard_map/dot_general | solution.py:63
  44.2 2.9 %convolution_convert_fusion.1 = bf16[112,512]{1,0:T(8,128)(2,1)S(1)} fusion(bf16[112,4096]{1,0:T(8,128)(2,1)S(1)} %all_gather.9, bf16[4096,512]{1,0:T(8,128)(2,1)} %param.12), kind=kOutput, calls=%fused_computation.19 | convolution fusion | flops 469819392 | bytes 5226496 | tf_op jit(solution)/shard_map/dot_general | solution.py:63
  47.2 6.4 %collective-permute-start.1 = (bf16[112,512]{1,0:T(8,128)(2,1)S(1)}, bf16[112,512]{1,0:T(8,128)(2,1)S(1)}, u32[]{:S(2)}, u32[]{:S(2)}) collective-permute-start(bf16[112,512]{1,0:T(8,128)(2,1)S(1)} %convolution_convert_fusion.1), channel_id=1, source_target_pairs={{4,0},{8,4},{12,8},{16,12},{20,16},{24,20},{28,24},{32,28},{36,32}... | collective-permute-start | bytes 344072 | tf_op jit(solution)/shard_map/ppermute | solution.py:14
  56.3 1.3 collective-permute-done.1
  57.8 65.8 %all-gather.3.cloned.1.call-done = bf16[7168,512]{1,0:T(8,128)(2,1)} async-done(((bf16[112,512]{1,0:T(8,128)(2,1)}), bf16[7168,512]{1,0:T(8,128)(2,1)}) %all-gather.3.cloned.1.call-update) | async-done | bytes 7340048 | tf_op jit(solution)/shard_map/all_gather | solution.py:91
  123.5 10.1 %copy.19 = bf16[7168,512]{0,1:T(8,128)(2,1)} copy(bf16[7168,512]{1,0:T(8,128)(2,1)} %all-gather.3.cloned.1.call-done) | data formatting | bytes 14680064
  133.6 33.0 %while.24 = (s32[]{:T(128)}, f32[4,224]{1,0:T(4,128)S(1)}, s32[]{:T(128)}, bf16[7168,512]{0,1:T(8,128)(2,1)}, bf16[224,4,128]{2,0,1:T(8,128)(2,1)S(1)}, /*index=...) while((s32[]{:T(128)}, f32[4,224]{1,0:T(4,128)S(1)}, s32[]{:T(128)}, ...), condition=%wide.region_7.8_spmd.clone, body=%wide.region_5.7_spmd.clone.sunk | while | flops 118932200 | bytes 2052007 | solution.py:103
  135.9 1.1 constant_dynamic-slice_fusion.6
  138.3 1.1 constant_dynamic-slice_fusion.6
  140.7 1.1 constant_dynamic-slice_fusion.6
  143.0 1.1 constant_dynamic-slice_fusion.6
  145.4 1.1 constant_dynamic-slice_fusion.6
  147.7 1.1 constant_dynamic-slice_fusion.6
  150.1 1.1 constant_dynamic-slice_fusion.6
  152.5 1.1 constant_dynamic-slice_fusion.6
  154.8 1.1 constant_dynamic-slice_fusion.6
  157.2 1.1 constant_dynamic-slice_fusion.6
  159.5 1.1 constant_dynamic-slice_fusion.6
  161.9 1.1 constant_dynamic-slice_fusion.6
  164.3 1.1 constant_dynamic-slice_fusion.6
  166.6 38.5 %all-gather.5.cloned.1.call-done = bf16[7168,512]{1,0:T(8,128)(2,1)} async-done(((bf16[112,512]{1,0:T(8,128)(2,1)}), bf16[7168,512]{1,0:T(8,128)(2,1)}) %all-gather.5.cloned.1.call-update) | async-done | bytes 7340048 | tf_op jit(solution)/shard_map/all_gather | solution.py:92
  205.2 60.7 %while.25 = (s32[]{:T(128)}, f32[4,224]{1,0:T(4,128)S(1)}, f32[4,224,128]{2,1,0:T(8,128)S(1)}, s32[]{:T(128)}, bf16[7168,512]{0,1:T(8,128)(2,1)}, /*index=5*/bf1...) while((s32[]{:T(128)}, f32[4,224]{1,0:T(4,128)S(1)}, ...), condition=%wide.region_10.11_spmd.clone, body=%wide.region_8.10_spmd.clone.sunk | while | flops 237404896 | bytes 7429571 | solution.py:112
  205.2 1.1 constant_dynamic-slice_fusion.7
  207.8 1.1 constant_dynamic-slice_fusion.8
  209.5 1.1 constant_dynamic-slice_fusion.7
  212.1 1.1 constant_dynamic-slice_fusion.8
  216.5 1.1 constant_dynamic-slice_fusion.8
  218.2 1.1 constant_dynamic-slice_fusion.7
  220.8 1.1 constant_dynamic-slice_fusion.8
  222.5 1.1 constant_dynamic-slice_fusion.7
  225.1 1.1 constant_dynamic-slice_fusion.8
  226.9 1.1 constant_dynamic-slice_fusion.7
  229.5 1.1 constant_dynamic-slice_fusion.8
  231.2 1.1 constant_dynamic-slice_fusion.7
  233.8 1.1 constant_dynamic-slice_fusion.8
  235.6 1.1 constant_dynamic-slice_fusion.7
  238.1 1.1 constant_dynamic-slice_fusion.8
  242.5 1.1 constant_dynamic-slice_fusion.8
  246.8 1.1 constant_dynamic-slice_fusion.8
  251.1 1.1 constant_dynamic-slice_fusion.8
  255.5 1.1 constant_dynamic-slice_fusion.8
  259.8 1.1 constant_dynamic-slice_fusion.8
  264.2 1.1 constant_dynamic-slice_fusion.8
  (202 shorter events, 62.0 us)
Async XLA Ops:
  6.5 117.0 %all-gather.3.cloned.1.call-start = ((), (), s32[]{:S(2)}) async-start(), calls=%async_computation | async-start | bytes 7454720 | tf_op jit(solution)/shard_map/all_gather | solution.py:91
  7.3 4.1 %collective-permute-start = (bf16[2,1024]{1,0:T(2,128)(2,1)S(1)}, bf16[2,1024]{1,0:T(2,128)(2,1)S(1)}, u32[]{:S(2)}, u32[]{:S(2)}) collective-permute-start(bf16[2,1024]{1,0:T(2,128)(2,1)S(1)} %slice.24), channel_id=1, source_target_pairs={{0,4},{4,8},{8,12},{12,16},{16,20},{20,24},{24,28},{28,32},{32,36}... | collective-permute-start | bytes 12296 | tf_op jit(solution)/shard_map/ppermute | solution.py:14
  35.9 7.3 %copy-start = (s32[64]{0:T(128)S(1)}, s32[64]{0:T(128)}, u32[]{:S(2)}) copy-start(s32[64]{0:T(128)} %param.15) | copy-start | bytes 772
  39.5 165.6 %all-gather.5.cloned.1.call-start = ((), (), s32[]{:S(2)}) async-start(), calls=%async_computation.1 | async-start | bytes 7454720 | tf_op jit(solution)/shard_map/all_gather | solution.py:92
  47.2 10.4 %collective-permute-start.1 = (bf16[112,512]{1,0:T(8,128)(2,1)S(1)}, bf16[112,512]{1,0:T(8,128)(2,1)S(1)}, u32[]{:S(2)}, u32[]{:S(2)}) collective-permute-start(bf16[112,512]{1,0:T(8,128)(2,1)S(1)} %convolution_convert_fusion.1), channel_id=1, source_target_pairs={{4,0},{8,4},{12,8},{16,12},{20,16},{24,20},{28,24},{32,28},{36,32}... | collective-permute-start | bytes 344072 | tf_op jit(solution)/shard_map/ppermute | solution.py:14
Sparse Core Ops, SparseCore 0:
  39.6 83.8 all-gather.2
  126.3 78.8 all-gather.4
where the time goes:
time: 277 us; the launch traced here: 274 us
  waiting for transfers between devices  106 us (38%)
  local copies, waits for them, and re-layouts  60.7 us (22%)
  matrix products  33.8 us (12%)
  other arithmetic  25.7 us (9%)
  blocking collectives  21.3 us (8%)
  between operations  15.4 us (6%)
  starting transfers between devices  9.67 us (3%)
    all_gather x1, waiting for transfers between devices, shards(): lax.all_gather(key_rows, 'seq', axis=0, tiled=True)  65.8 us
    all_gather x1, waiting for transfers between devices, shards(): lax.all_gather(value_rows, 'seq', axis=0, tiled=True)  38.5 us
    dynamic_slice x28, local copies, waits for them, and re-layouts, add_block(): value_block = lax.dynamic_slice_in_dim(value_all, offset, block_size, 0)  18.1 us
    dot_general x28, matrix products, block_scores(): jnp.einsum('qhd,khd->hqk', owned, keyed, preferred_element_type=jnp.float32)  17.6 us
    add x28, other arithmetic, shards(): query_pos = first_row + jnp.arange(capacity, dtype=jnp.int32)  16.1 us
    dynamic_slice x14, local copies, waits for them, and re-layouts, find_max(): lax.dynamic_slice_in_dim(key_all, index * block_size, block_size, 0)  15.2 us
    dynamic_slice x14, local copies, waits for them, and re-layouts, add_block(): key_block = lax.dynamic_slice_in_dim(key_all, offset, block_size, 0)  15.1 us
    all_gather x1, blocking collectives, shards(): shard_rows = lax.all_gather(coarse_part, 'head', axis=1, tiled=True)  12.6 us
  transfers between devices with their start and end apart: 4, of which 3 were waited for; matrix products, arithmetic and copies ran while one was open for 19% of the time, Pallas kernels for 0%

commit v1 on v0

--- a/solution.py
+++ b/solution.py
@@ -6,6 +6,13 @@
 
 HD = 128
 masked_score = -1e30
+
+
+def gather_over(block, mesh_axis, along):
+    count = lax.axis_size(mesh_axis)
+    shards = jnp.stack([block for _ in range(count)])
+    shards = lax.all_to_all(shards, mesh_axis, split_axis=0, concat_axis=0)
+    return jnp.concatenate(shards, axis=along)
 
 
 def from_behind(x, axis, by):
@@ -88,7 +95,7 @@
         jnp.zeros((head_count, capacity, HD), jnp.float32),
     )
     key_all, value_all = (
-        lax.all_gather(key_rows, "seq", axis=0, tiled=True),
+        gather_over(key_rows, "seq", 0),
         lax.all_gather(value_rows, "seq", axis=0, tiled=True),
     )
     block_size = math.gcd(coarse_total, 512)

time: 277 us -> 357 us (1.29)
  waiting for transfers between devices: 106 us -> 169 us
  starting transfers between devices: 9.67 us -> 21.5 us
  local copies, waits for them, and re-layouts: 60.7 us -> 64.6 us
    ppermute x2, waiting for transfers between devices: 1.29 us -> 169 us  [from_behind(): return lax.ppermute(x, axis, pairs)]
    all_gather x1 -> x0, waiting for transfers between devices: 65.8 us -> none  [shards(): lax.all_gather(key_rows, 'seq', axis=0, tiled=True)]
    all_gather x1, waiting for transfers between devices: 38.5 us -> 0.02 us  [shards(): lax.all_gather(value_rows, 'seq', axis=0, tiled=True)]
    all_to_all x0 -> x1, starting transfers between devices: none -> 16 us  [gather_over(): shards = lax.all_to_all(shards, mesh_axis, split_axis=0, concat_axis=0)]
    ppermute x2, starting transfers between devices: 9.63 us -> 5.45 us  [from_behind(): return lax.ppermute(x, axis, pairs)]
    another operation x1 -> x2, local copies, waits for them, and re-layouts: 0.1 us -> 4.01 us  [the longest x1 3.91 us: gather_over(): shards = jnp.stack([block for _ in range(count)])]
  transfers between devices with their start and end apart: 4 -> 4, of which waited for: 3 -> 1; matrix products, arithmetic and copies ran while one was open for 19% -> 15% of each run, Pallas kernels for 0% -> 0%
where the time goes in v1:
time: 357 us; the launch traced here: 354 us
  waiting for transfers between devices  169 us (47%)
  local copies, waits for them, and re-layouts  64.6 us (18%)
  matrix products  33.1 us (9%)
  other arithmetic  27.4 us (8%)
  starting transfers between devices  21.5 us (6%)
  blocking collectives  21.3 us (6%)
  between operations  15.5 us (4%)
    ppermute x2, waiting for transfers between devices, from_behind(): return lax.ppermute(x, axis, pairs)  169 us
    dynamic_slice x28, local copies, waits for them, and re-layouts, add_block(): value_block = lax.dynamic_slice_in_dim(value_all, offset, block_size, 0)  18.1 us
    add x28, other arithmetic, shards(): query_pos = first_row + jnp.arange(capacity, dtype=jnp.int32)  17.9 us
    dot_general x28, matrix products, block_scores(): jnp.einsum('qhd,khd->hqk', owned, keyed, preferred_element_type=jnp.float32)  17.6 us
    all_to_all x1, starting transfers between devices, gather_over(): shards = lax.all_to_all(shards, mesh_axis, split_axis=0, concat_axis=0)  16 us
    dynamic_slice x14, local copies, waits for them, and re-layouts, add_block(): key_block = lax.dynamic_slice_in_dim(key_all, offset, block_size, 0)  15.1 us
    dynamic_slice x14, local copies, waits for them, and re-layouts, find_max(): lax.dynamic_slice_in_dim(key_all, index * block_size, block_size, 0)  15.1 us
    all_gather x1, blocking collectives, shards(): shard_rows = lax.all_gather(coarse_part, 'head', axis=1, tiled=True)  12.6 us
  transfers between devices with their start and end apart: 4, of which 1 were waited for; matrix products, arithmetic and copies ran while one was open for 15% of the time, Pallas kernels for 0%

profile of v1, /device:TPU:199, one launch (start us, length us, event | category | flops | bytes accessed | tf_op | source)
XLA Modules:
  0.0 353.7 jit_solution(13786191954985210566)
XLA Ops:
  7.3 3.2 collective-permute-start
  11.3 1.3 pad_maximum_fusion
  14.4 8.7 %psum.7 = f32[112]{0:T(128)S(1)} all-reduce(f32[112]{0:T(128)S(1)} %get-tuple-element.190), channel_id=1, replica_groups=mesh['seq'=64,'head'=4] {'head'}, use_global_device_ids=true, to_apply=%region_4.5 | all-reduce | flops 112 | bytes 896 | tf_op jit(solution)/shard_map/psum | solution.py:60
  23.3 12.6 %all_gather.6 = bf16[112,4096]{1,0:T(8,128)(2,1)S(1)} all-gather(bf16[112,1024]{1,0:T(8,128)(2,1)S(1)} %multiply_convert_fusion), channel_id=1, replica_groups=mesh['seq'=64,'head'=4] {'head'}, dimensions={1}, use_global_device_ids=true | all-gather | bytes 1146880 | tf_op jit(solution)/shard_map/all_gather | solution.py:67
  35.9 2.9 convolution_convert_fusion.2
  38.8 3.9 %stack.2 = bf16[64,112,512]{2,1,0:T(8,128)(2,1)} broadcast(bf16[112,512]{1,0:T(8,128)(2,1)S(1)} %convolution_convert_fusion.2), dimensions={1,2} | broadcast | bytes 7454720 | tf_op jit(solution)/shard_map/stack | solution.py:13
  42.7 16.0 %all-to-all-start = ((bf16[64,112,512]{2,1,0:T(8,128)(2,1)}), bf16[64,112,512]{2,1,0:T(8,128)(2,1)}, u32[]{:S(2)}, u32[]{:S(2)}) async-start(bf16[64,112,512]{2,1,0:T(8,128)(2,1)} %stack.2), calls=%async_computation | async-start | bytes 14680064 | tf_op jit(solution)/shard_map/all_to_all | solution.py:14
  58.8 3.6 %convolution_convert_fusion = bf16[112,512]{1,0:T(8,128)(2,1)} fusion(bf16[112,4096]{1,0:T(8,128)(2,1)S(1)} %all_gather.6, bf16[4096,512]{1,0:T(8,128)(2,1)} %param.14), kind=kOutput, calls=%fused_computation.18 | convolution fusion | flops 469819392 | bytes 5226496 | tf_op jit(solution)/shard_map/dot_general | solution.py:70
  63.4 2.9 convolution_convert_fusion.1
  66.4 2.3 collective-permute-start.1
  71.3 168.7 %collective-permute-done.1 = bf16[112,512]{1,0:T(8,128)(2,1)S(1)} collective-permute-done((bf16[112,512]{1,0:T(8,128)(2,1)S(1)}, bf16[112,512]{1,0:T(8,128)(2,1)S(1)}, u32[]{:S(2)}, u32[]{:S(2)}) %collective-permute-start.1) | collective-permute-done | bytes 114720 | tf_op jit(solution)/shard_map/ppermute | solution.py:21
  240.3 10.1 %copy.30 = bf16[7168,512]{0,1:T(8,128)(2,1)} copy(bf16[7168,512]{1,0:T(8,128)(2,1)} %bitcast.6) | data formatting | bytes 14680064
  250.3 33.9 %while.24 = (s32[]{:T(128)}, f32[4,224]{1,0:T(4,128)S(1)}, s32[]{:T(128)}, bf16[7168,512]{0,1:T(8,128)(2,1)}, bf16[224,4,128]{2,0,1:T(8,128)(2,1)S(1)}, /*index=...) while((s32[]{:T(128)}, f32[4,224]{1,0:T(4,128)S(1)}, s32[]{:T(128)}, ...), condition=%wide.region_7.8_spmd.clone, body=%wide.region_5.7_spmd.clone.sunk | while | flops 118932200 | bytes 2052007 | solution.py:110
  252.7 1.1 constant_dynamic-slice_fusion.6
  255.2 1.1 constant_dynamic-slice_fusion.6
  257.6 1.1 constant_dynamic-slice_fusion.6
  260.0 1.1 constant_dynamic-slice_fusion.6
  262.4 1.1 constant_dynamic-slice_fusion.6
  264.8 1.1 constant_dynamic-slice_fusion.6
  267.3 1.1 constant_dynamic-slice_fusion.6
  269.7 1.1 constant_dynamic-slice_fusion.6
  272.1 1.1 constant_dynamic-slice_fusion.6
  274.5 1.1 constant_dynamic-slice_fusion.6
  277.0 1.1 constant_dynamic-slice_fusion.6
  281.8 1.1 constant_dynamic-slice_fusion.6
  284.3 61.6 %while.25 = (s32[]{:T(128)}, f32[4,224]{1,0:T(4,128)S(1)}, f32[4,224,128]{2,1,0:T(8,128)S(1)}, s32[]{:T(128)}, bf16[7168,512]{0,1:T(8,128)(2,1)}, /*index=5*/bf1...) while((s32[]{:T(128)}, f32[4,224]{1,0:T(4,128)S(1)}, ...), condition=%wide.region_10.11_spmd.clone, body=%wide.region_8.10_spmd.clone.sunk | while | flops 237404896 | bytes 7429571 | solution.py:119
  284.3 1.1 constant_dynamic-slice_fusion.7
  287.0 1.1 constant_dynamic-slice_fusion.8
  288.7 1.1 constant_dynamic-slice_fusion.7
  291.4 1.1 constant_dynamic-slice_fusion.8
  293.1 1.1 constant_dynamic-slice_fusion.7
  295.8 1.1 constant_dynamic-slice_fusion.8
  297.5 1.1 constant_dynamic-slice_fusion.7
  300.2 1.1 constant_dynamic-slice_fusion.8
  301.9 1.1 constant_dynamic-slice_fusion.7
  304.6 1.1 constant_dynamic-slice_fusion.8
  306.3 1.1 constant_dynamic-slice_fusion.7
  309.0 1.1 constant_dynamic-slice_fusion.8
  310.7 1.1 constant_dynamic-slice_fusion.7
  313.4 1.1 constant_dynamic-slice_fusion.8
  315.1 1.1 constant_dynamic-slice_fusion.7
  317.8 1.1 constant_dynamic-slice_fusion.8
  322.2 1.1 constant_dynamic-slice_fusion.8
  326.6 1.1 constant_dynamic-slice_fusion.8
  331.0 1.1 constant_dynamic-slice_fusion.8
  335.4 1.1 constant_dynamic-slice_fusion.8
  339.8 1.1 constant_dynamic-slice_fusion.8
  344.2 1.1 constant_dynamic-slice_fusion.8
  (202 shorter events, 63.7 us)
Async XLA Ops:
  7.3 4.1 %collective-permute-start = (bf16[2,1024]{1,0:T(2,128)(2,1)S(1)}, bf16[2,1024]{1,0:T(2,128)(2,1)S(1)}, u32[]{:S(2)}, u32[]{:S(2)}) collective-permute-start(bf16[2,1024]{1,0:T(2,128)(2,1)S(1)} %slice.24), channel_id=1, source_target_pairs={{0,4},{4,8},{8,12},{12,16},{16,20},{20,24},{24,28},{28,32},{32,36}... | collective-permute-start | bytes 12296 | tf_op jit(solution)/shard_map/ppermute | solution.py:21
  42.7 197.5 %all-to-all-start = ((bf16[64,112,512]{2,1,0:T(8,128)(2,1)}), bf16[64,112,512]{2,1,0:T(8,128)(2,1)}, u32[]{:S(2)}, u32[]{:S(2)}) async-start(bf16[64,112,512]{2,1,0:T(8,128)(2,1)} %stack.2), calls=%async_computation | async-start | bytes 14680064 | tf_op jit(solution)/shard_map/all_to_all | solution.py:14
  58.7 3.7 %copy-start = (s32[64]{0:T(128)S(1)}, s32[64]{0:T(128)}, u32[]{:S(2)}) copy-start(s32[64]{0:T(128)} %param.15) | copy-start | bytes 772
  58.7 225.5 %all-gather.2.cloned.1.call-start = ((), (), s32[]{:S(2)}) async-start(), calls=%async_computation.1 | async-start | bytes 7454720 | tf_op jit(solution)/shard_map/all_gather | solution.py:99
  66.4 173.7 %collective-permute-start.1 = (bf16[112,512]{1,0:T(8,128)(2,1)S(1)}, bf16[112,512]{1,0:T(8,128)(2,1)S(1)}, u32[]{:S(2)}, u32[]{:S(2)}) collective-permute-start(bf16[112,512]{1,0:T(8,128)(2,1)S(1)} %convolution_convert_fusion.1), channel_id=1, source_target_pairs={{4,0},{8,4},{12,8},{16,12},{20,16},{24,20},{28,24},{32,28},{36,32}... | collective-permute-start | bytes 344072 | tf_op jit(solution)/shard_map/ppermute | solution.py:21
Sparse Core Ops, SparseCore 0:
  62.5 119.0 all-gather.1
